TPU v7x, 128 devices: a whole 4x4x4 slice. The times are simulated.
128 devices in a mesh: seq: 32 (over x_hi, z, y), tensor: 2 (over core), dp: 2 (over x_lo).
Axes of the slice: x: 4 (x_hi: 2, x_lo: 2; x = x_hi * 2 + x_lo), y: 4, z: 4, core: 2. Of those that a mesh axis runs over, the one named last changes fastest.
Arguments:
- inputs: bfloat16 [2, 24576, 1536], P('dp', 'seq', 'tensor'), may hold values from -6 to 6
- lengths: int32 [2], P('dp'), may hold values from 6144 to 24576, as said below
- cotangent: bfloat16 [2, 24576, 1536], P('dp', 'seq', 'tensor'), may hold values from -6 to 6
- w_value: bfloat16 [1536, 1536], P(None, 'tensor'), may hold values from -0.15625 to 0.15625
- w_gate: bfloat16 [1536, 1536], P(None, 'tensor'), may hold values from -0.15625 to 0.15625
- kernel: bfloat16 [31, 1536], P(None, 'tensor'), may hold values from -1 to 1
- w_out: bfloat16 [1536, 1536], P('tensor'), may hold values from -0.15625 to 0.15625
Outputs:
- output: bfloat16 [2, 24576, 1536], P('dp', 'seq', 'tensor')
- input_gradient: bfloat16 [2, 24576, 1536], P('dp', 'seq', 'tensor')
- value_grad: float32 [1536, 1536], P(('seq', 'dp'), 'tensor')
- gate_grad: float32 [1536, 1536], P(('seq', 'dp'), 'tensor')
- kernel_grad: float32 [31, 1536], P(None, 'tensor')
- out_grad: float32 [1536, 1536], P('tensor', ('seq', 'dp'))
Inputs may be any that keep to these rules, and one draw needn't show every extreme that they name: `lengths`: in every draw some utterance has all 24576 frames valid.
All inputs are finite; a program needn't handle non-finite values.
Results may differ from a plain program's by a relative error of at most 0.009.
Values may be sent and summed in bfloat16 or wider, within the bound.
A program may use at most 128 MiB of HBM per device.

v0:
```python
import jax
import jax.numpy as jnp
from jax import lax
from jax.sharding import PartitionSpec as P

epsilon = 1e-05


def padded_2(shard, sides, width):
    for axis, dim in sides:
        peers, length = (lax.axis_size(axis), shard.shape[dim])
        up = [(i, (i + 1) % peers) for i in range(peers - 1)]
        down = [(j, i) for i, j in up]
        last = lax.slice_in_dim(shard, length - width, length, axis=dim)
        leading = lax.slice_in_dim(shard, 0, width, axis=dim)
        before = lax.ppermute(last, axis, up)
        after = lax.ppermute(leading, axis, down)
        shard = jnp.concatenate([before, shard, after], axis=dim)
    return shard


def layer_normalizer(values):
    center = values - jnp.mean(values, axis=-1, keepdims=True)
    inverse = lax.rsqrt(jnp.mean(center * center, axis=-1, keepdims=True) + epsilon)
    return (center * inverse, inverse)


def shards(inputs, lengths, cotangent, w_value, w_gate, kernel, w_out):
    frame_total = inputs[0]
    count = frame_total.shape[0]
    channel_total = frame_total.shape[1]
    channel_width = channel_total * lax.axis_size("tensor")
    taps_count = kernel.shape[0]
    half = (taps_count - 1) // 2
    tensor_position = lax.axis_index("tensor")
    first_frame = lax.axis_index("seq") * count
    positions = first_frame + jnp.arange(count, dtype=jnp.int32)
    valid = (positions < lengths[0]).astype(jnp.float32)[:, None]
    taps = kernel.astype(jnp.float32)
    complete_rows = lax.all_gather(frame_total, "tensor", axis=1, tiled=True)
    centered_scaled, inverse_deviation_one = layer_normalizer(complete_rows.astype(jnp.float32))
    normalized_rows = centered_scaled.astype(jnp.bfloat16)
    values = jnp.dot(normalized_rows, w_value, preferred_element_type=jnp.float32)
    gates = jnp.dot(normalized_rows, w_gate, preferred_element_type=jnp.float32)
    sigma = jax.nn.sigmoid(gates)
    hidden = (values * sigma * valid).astype(jnp.bfloat16)
    padded = padded_2(hidden, (("seq", 0),), half).astype(jnp.float32)
    conv = jnp.zeros((count, channel_total), jnp.float32)
    for offset in range(taps_count):
        conv = conv + padded[offset : offset + count] * taps[offset]
    conv_sum, conv_square = lax.psum(
        (jnp.sum(conv, axis=-1), jnp.sum(conv * conv, axis=-1)), "tensor"
    )
    conv_mean = (conv_sum / channel_width)[:, None]
    conv_var = (conv_square / channel_width)[:, None] - conv_mean * conv_mean
    rstd_two = lax.rsqrt(conv_var + epsilon)
    zhat = (conv - conv_mean) * rstd_two
    swish_gate = jax.nn.sigmoid(zhat)
    swished = (zhat * swish_gate).astype(jnp.bfloat16)
    partial_out = jnp.dot(swished, w_out, preferred_element_type=jnp.float32)
    summed = lax.psum_scatter(
        partial_out.astype(jnp.bfloat16), "tensor", scatter_dimension=1, tiled=True
    ).astype(jnp.float32)
    output = (frame_total.astype(jnp.float32) + summed).astype(jnp.bfloat16)
    upstream = cotangent[0]
    upstream_whole = lax.all_gather(upstream, "tensor", axis=1, tiled=True)
    out_term = jnp.dot(swished.T, upstream_whole, preferred_element_type=jnp.float32)
    dswish = jnp.dot(upstream_whole, w_out.T, preferred_element_type=jnp.float32)
    dswish = dswish * (swish_gate + zhat * swish_gate * (1.0 - swish_gate))
    slope_sum, slope_cross = lax.psum(
        (jnp.sum(dswish, axis=-1), jnp.sum(dswish * zhat, axis=-1)), "tensor"
    )
    dconv = rstd_two * (
        dswish
        - (slope_sum / channel_width)[:, None]
        - zhat * (slope_cross / channel_width)[:, None]
    )
    dconv = dconv.astype(jnp.bfloat16)
    slope = dconv.astype(jnp.float32)
    kernel_term = jnp.stack(
        [jnp.sum(padded[offset : offset + count] * slope, axis=0) for offset in range(taps_count)]
    )
    slope_pad = padded_2(dconv, (("seq", 0),), half).astype(jnp.float32)
    dhidden = jnp.zeros((count, channel_total), jnp.float32)
    for offset in range(taps_count):
        dhidden = dhidden + slope_pad[2 * half - offset : 2 * half - offset + count] * taps[offset]
    dhidden = dhidden * valid
    dvalues = (dhidden * sigma).astype(jnp.bfloat16)
    dgates = (dhidden * values * sigma * (1.0 - sigma)).astype(jnp.bfloat16)
    value_term = jnp.dot(normalized_rows.T, dvalues, preferred_element_type=jnp.float32)
    gate_term = jnp.dot(normalized_rows.T, dgates, preferred_element_type=jnp.float32)
    kernel_grad = lax.psum(kernel_term, ("seq", "dp"))
    dnormed_part = jnp.dot(dvalues, w_value.T, preferred_element_type=jnp.float32) + jnp.dot(
        dgates, w_gate.T, preferred_element_type=jnp.float32
    )
    normalized_grad = lax.psum_scatter(
        dnormed_part.astype(jnp.bfloat16), "tensor", scatter_dimension=1, tiled=True
    ).astype(jnp.float32)
    local_centered_scaled = lax.dynamic_slice_in_dim(
        centered_scaled, tensor_position * channel_total, channel_total, 1
    )
    input_total_sum, input_cross_term = lax.psum(
        (
            jnp.sum(normalized_grad, axis=-1),
            jnp.sum(normalized_grad * local_centered_scaled, axis=-1),
        ),
        "tensor",
    )
    input_gradient = upstream.astype(jnp.float32) + inverse_deviation_one * (
        normalized_grad
        - (input_total_sum / channel_width)[:, None]
        - local_centered_scaled * (input_cross_term / channel_width)[:, None]
    )
    input_gradient = input_gradient.astype(jnp.bfloat16)
    value_grad, gate_grad, out_grad = (
        lax.psum_scatter(value_term, ("seq", "dp"), scatter_dimension=0, tiled=True),
        lax.psum_scatter(gate_term, ("seq", "dp"), scatter_dimension=0, tiled=True),
        lax.psum_scatter(out_term, ("seq", "dp"), scatter_dimension=1, tiled=True),
    )
    return (output[None], input_gradient[None], value_grad, gate_grad, kernel_grad, out_grad)


def solution(mesh):
    return jax.shard_map(
        shards,
        mesh=mesh,
        in_specs=(
            P("dp", "seq", "tensor"),
            P("dp"),
            P("dp", "seq", "tensor"),
            P(None, "tensor"),
            P(None, "tensor"),
            P(None, "tensor"),
            P("tensor", None),
        ),
        out_specs=(
            P("dp", "seq", "tensor"),
            P("dp", "seq", "tensor"),
            P(("seq", "dp"), "tensor"),
            P(("seq", "dp"), "tensor"),
            P(None, "tensor"),
            P("tensor", ("seq", "dp")),
        ),
        check_vma=False,
    )
```

profile of v0, /device:TPU:0, one launch (start us, length us, event | category | flops | bytes accessed | tf_op | source)
XLA Modules:
  0.0 1369.6 jit_solution(1484095070607599668)
XLA Ops:
  9.8 16.1 %all-gather.5.cloned.1.call-done = bf16[1,768,1536]{2,1,0:T(8,128)(2,1)} async-done(((bf16[1,768,768]{2,1,0:T(8,128)(2,1)}), bf16[1,768,1536]{2,1,0:T(8,128)(2,1)}) %all-gather.5.cloned.1.call-update) | async-done | bytes 2359312 | tf_op jit(solution)/shard_map/all_gather | solution.py:40
  31.4 3.5 multiply_convert_fusion.3
  34.9 3.5 collective-permute-start
  39.9 4.2 collective-permute-done.1
  44.5 10.7 fusion.94
  57.9 7.0 fusion.93
  67.5 27.0 %fusion.39 = (f32[768]{0:T(1024)}, f32[768]{0:T(1024)}, f32[768]{0:T(1024)}, f32[768]{0:T(1024)}, f32[768]{0:T(1024)}, /*index=5*/f32[768]{0:T(1024)}, f32[768]{...) fusion(f32[798,768]{1,0:T(8,128)} %copy-done.1, ...), kind=kLoop, calls=%fused_computation.77 | loop fusion | flops 25938432 | bytes 48433152 | tf_op jit(solution)/shard_map/reduce_sum | solution.py:81
  95.1 4.0 collective-permute-start.2
  100.4 3.9 convolution_convert_fusion
  106.5 10.9 multiply_convert_fusion
  119.9 3.5 add_convert_fusion
  123.9 15.4 %fusion.38 = (f32[768]{0:T(1024)S(1)}, f32[768]{0:T(1024)S(1)}, f32[768]{0:T(1024)S(1)}, f32[768]{0:T(1024)S(1)}, f32[768]{0:T(1024)S(1)}, /*index=5*/f32[768]{0...) fusion(bf16[768,768]{1,0:T(8,128)(2,1)S(1)} %get-tuple-element., ...), kind=kLoop, calls=%fused_computation.76 | loop fusion | flops 15915264 | bytes 31890432 | tf_op jit(solution)/shard_map/reduce_sum | solution.py:81
  139.9 2.6 stack.127
  142.6 7.1 fusion.72
  151.0 6.1 fusion.88
  158.3 6.1 fusion.86
  164.5 4.4 fusion.1
  171.6 2.6 convert_reduce_fusion.1
  174.2 3.1 all-reduce
  177.9 3.6 fusion.81
  181.6 95.1 %all-reduce.5.cloned.1.call-done = f32[31,768]{1,0:T(8,128)} async-done(((f32[31,768]{1,0:T(8,128)}), f32[31,768]{1,0:T(8,128)}) %all-reduce.5.cloned.1.call-update) | async-done | bytes 95248 | tf_op jit(solution)/shard_map/psum | solution.py:92
  276.7 363.2 %reduce-scatter.14.cloned.1.call-done = f32[768,24]{0,1:T(8,128)} async-done(((f32[768,1536]{0,1:T(8,128)}), f32[768,24]{0,1:T(8,128)}) %reduce-scatter.14.cloned.1.call-update) | async-done | bytes 73744 | tf_op jit(solution)/shard_map/reduce_scatter | solution.py:118
  639.9 360.7 %reduce-scatter.10.cloned.1.call-done = f32[24,768]{1,0:T(8,128)} async-done(((f32[1536,768]{1,0:T(8,128)}), f32[24,768]{1,0:T(8,128)}) %reduce-scatter.10.cloned.1.call-update) | async-done | bytes 73744 | tf_op jit(solution)/shard_map/reduce_scatter | solution.py:116
  1000.6 360.6 %reduce-scatter.12.cloned.1.call-done = f32[24,768]{1,0:T(8,128)} async-done(((f32[1536,768]{1,0:T(8,128)}), f32[24,768]{1,0:T(8,128)}) %reduce-scatter.12.cloned.1.call-update) | async-done | bytes 73744 | tf_op jit(solution)/shard_map/reduce_scatter | solution.py:117
  (274 shorter events, 28.0 us)
Async XLA Ops:
  7.2 18.6 %all-gather.5.cloned.1.call-start = ((), (), s32[]{:S(2)}) async-start(), calls=%async_computation.11 | async-start | bytes 3538944 | tf_op jit(solution)/shard_map/all_gather | solution.py:40
  7.9 50.0 %all-gather.7.cloned.1.call-start = ((), (), s32[]{:S(2)}) async-start(), calls=%async_computation.12 | async-start | bytes 3538944 | tf_op jit(solution)/shard_map/all_gather | solution.py:66
  8.7 160.3 %reduce-scatter.6.cloned.1.call-start = ((), (), s32[]{:S(2)}) async-start(), calls=%async_computation.5 | async-start | bytes 3538944 | tf_op jit(solution)/shard_map/reduce_scatter | solution.py:61
  9.6 34.8 %copy-start.13 = (f32[768]{0:T(1024)}, f32[768]{0:T(1024)S(1)}, u32[]{:S(2)}) copy-start(f32[768]{0:T(1024)S(1)} %get-tuple-element.47) | copy-start | bytes 9220
  9.6 34.8 %copy-start.15 = (f32[768]{0:T(1024)}, f32[768]{0:T(1024)S(1)}, u32[]{:S(2)}) copy-start(f32[768]{0:T(1024)S(1)} %get-tuple-element.48) | copy-start | bytes 9220
  9.6 34.8 %copy-start.17 = (f32[768]{0:T(1024)}, f32[768]{0:T(1024)S(1)}, u32[]{:S(2)}) copy-start(f32[768]{0:T(1024)S(1)} %get-tuple-element.49) | copy-start | bytes 9220
  9.6 34.8 %copy-start.19 = (f32[768]{0:T(1024)}, f32[768]{0:T(1024)S(1)}, u32[]{:S(2)}) copy-start(f32[768]{0:T(1024)S(1)} %get-tuple-element.50) | copy-start | bytes 9220
  9.6 34.8 %copy-start.21 = (f32[768]{0:T(1024)}, f32[768]{0:T(1024)S(1)}, u32[]{:S(2)}) copy-start(f32[768]{0:T(1024)S(1)} %get-tuple-element.51) | copy-start | bytes 9220
  9.6 34.8 %copy-start.23 = (f32[768]{0:T(1024)}, f32[768]{0:T(1024)S(1)}, u32[]{:S(2)}) copy-start(f32[768]{0:T(1024)S(1)} %get-tuple-element.52) | copy-start | bytes 9220
  9.6 34.8 %copy-start.25 = (f32[768]{0:T(1024)}, f32[768]{0:T(1024)S(1)}, u32[]{:S(2)}) copy-start(f32[768]{0:T(1024)S(1)} %get-tuple-element.53) | copy-start | bytes 9220
  9.6 34.8 %copy-start.27 = (f32[768]{0:T(1024)}, f32[768]{0:T(1024)S(1)}, u32[]{:S(2)}) copy-start(f32[768]{0:T(1024)S(1)} %get-tuple-element.54) | copy-start | bytes 9220
  9.7 34.8 %copy-start.29 = (f32[768]{0:T(1024)}, f32[768]{0:T(1024)S(1)}, u32[]{:S(2)}) copy-start(f32[768]{0:T(1024)S(1)} %get-tuple-element.55) | copy-start | bytes 9220
  9.7 34.8 %copy-start.31 = (f32[768]{0:T(1024)}, f32[768]{0:T(1024)S(1)}, u32[]{:S(2)}) copy-start(f32[768]{0:T(1024)S(1)} %get-tuple-element.56) | copy-start | bytes 9220
  9.7 34.8 %copy-start.33 = (f32[768]{0:T(1024)}, f32[768]{0:T(1024)S(1)}, u32[]{:S(2)}) copy-start(f32[768]{0:T(1024)S(1)} %get-tuple-element.57) | copy-start | bytes 9220
  9.7 34.8 %copy-start.35 = (f32[768]{0:T(1024)}, f32[768]{0:T(1024)S(1)}, u32[]{:S(2)}) copy-start(f32[768]{0:T(1024)S(1)} %get-tuple-element.58) | copy-start | bytes 9220
  34.9 5.0 collective-permute-start
  38.4 5.7 collective-permute-start.1
  95.1 9.5 collective-permute-start.2
  99.0 6.0 collective-permute-start.3
  104.3 67.3 %reduce-scatter.8.cloned.1.call-start = ((), (), s32[]{:S(2)}) async-start(), calls=%async_computation.6 | async-start | bytes 3538944 | tf_op jit(solution)/shard_map/reduce_scatter | solution.py:96
  123.5 153.2 %all-reduce.5.cloned.1.call-start = ((), (), s32[]{:S(2)}) async-start(), calls=%async_computation.9 | async-start | bytes 196608 | tf_op jit(solution)/shard_map/psum | solution.py:92
  142.5 497.4 %reduce-scatter.14.cloned.1.call-start = ((), (), s32[]{:S(2)}) async-start(), calls=%async_computation.10 | async-start | bytes 4792320 | tf_op jit(solution)/shard_map/reduce_scatter | solution.py:118
  149.8 850.8 %reduce-scatter.10.cloned.1.call-start = ((), (), s32[]{:S(2)}) async-start(), calls=%async_computation.7 | async-start | bytes 4792320 | tf_op jit(solution)/shard_map/reduce_scatter | solution.py:116
  157.1 1204.1 %reduce-scatter.12.cloned.1.call-start = ((), (), s32[]{:S(2)}) async-start(), calls=%async_computation.8 | async-start | bytes 4792320 | tf_op jit(solution)/shard_map/reduce_scatter | solution.py:117
  (86 other events, 871.8 us)
Sparse Core Ops, SparseCore 0:
  9.7 16.1 all-gather.4
  27.5 14.9 all-gather.6
  104.4 19.5 reduce-scatter.5
  126.2 18.9 reduce-scatter.7
  150.3 126.3 all-reduce.4
  279.5 360.3 reduce-scatter.13
  642.9 357.6 reduce-scatter.9
  1003.5 357.6 reduce-scatter.11
where the time goes:
time: 1370 us
  waiting for transfers between devices  1200 us (88%)
  other arithmetic  82.8 us (6%)
  matrix products  41.6 us (3%)
  between operations  16.6 us (1%)
    reduce_scatter x1, waiting for transfers between devices, shards(): lax.psum_scatter(out_term, ('seq', 'dp'), scatter_dimension=1, tiled=True)  363 us
    reduce_scatter x1, waiting for transfers between devices, shards(): lax.psum_scatter(value_term, ('seq', 'dp'), scatter_dimension=0, tiled=True)  361 us
    reduce_scatter x1, waiting for transfers between devices, shards(): lax.psum_scatter(gate_term, ('seq', 'dp'), scatter_dimension=0, tiled=True)  361 us
    psum x1, waiting for transfers between devices, shards(): kernel_grad = lax.psum(kernel_term, ('seq', 'dp'))  95.1 us
    reduce_sum x2, other arithmetic, shards(): jnp.sum(padded[offset:offset + count] * slope, axis=0)  42.4 us
  transfers between devices with their start and end apart: 12, of which 7 were waited for; matrix products, arithmetic and copies ran while one was open for 7% of the time, Pallas kernels for 0%

commit v1 on v0

--- a/solution.py
+++ b/solution.py
@@ -89,7 +89,7 @@
     dgates = (dhidden * values * sigma * (1.0 - sigma)).astype(jnp.bfloat16)
     value_term = jnp.dot(normalized_rows.T, dvalues, preferred_element_type=jnp.float32)
     gate_term = jnp.dot(normalized_rows.T, dgates, preferred_element_type=jnp.float32)
-    kernel_grad = lax.psum(kernel_term, ("seq", "dp"))
+    kernel_grad = lax.psum(lax.psum(kernel_term, "dp"), "seq")
     dnormed_part = jnp.dot(dvalues, w_value.T, preferred_element_type=jnp.float32) + jnp.dot(
         dgates, w_gate.T, preferred_element_type=jnp.float32
     )

time: 1370 us -> 1600 us (1.17)
  waiting for transfers between devices: 1200 us -> 1420 us
  local copies, waits for them, and re-layouts: 8.21 us -> 30.4 us
    psum x1 -> x2, waiting for transfers between devices: 95.1 us -> 315 us  [shards(): kernel_grad = lax.psum(lax.psum(kernel_term, 'dp'), 'seq')]
    another operation x32, local copies, waits for them, and re-layouts: 2.72 us -> 23.7 us  [shards(): jnp.stack([jnp.sum(padded[offset:offset + count] * slope, axis=0) for off...]
  transfers between devices with their start and end apart: 12 -> 13, of which waited for: 7 -> 8; matrix products, arithmetic and copies ran while one was open for 7% -> 5% of each run, Pallas kernels for 0% -> 0%
where the time goes in v1:
time: 1600 us
  waiting for transfers between devices  1420 us (89%)
  other arithmetic  70.5 us (4%)
  matrix products  43.8 us (3%)
  local copies, waits for them, and re-layouts  30.4 us (2%)
    reduce_scatter x1, waiting for transfers between devices, shards(): lax.psum_scatter(out_term, ('seq', 'dp'), scatter_dimension=1, tiled=True)  365 us
    reduce_scatter x1, waiting for transfers between devices, shards(): lax.psum_scatter(gate_term, ('seq', 'dp'), scatter_dimension=0, tiled=True)  361 us
    reduce_scatter x1, waiting for transfers between devices, shards(): lax.psum_scatter(value_term, ('seq', 'dp'), scatter_dimension=0, tiled=True)  361 us
    psum x2, waiting for transfers between devices, shards(): kernel_grad = lax.psum(lax.psum(kernel_term, 'dp'), 'seq')  315 us
  transfers between devices with their start and end apart: 13, of which 8 were waited for; matrix products, arithmetic and copies ran while one was open for 5% of the time, Pallas kernels for 0%

profile of v1, /device:TPU:0, one launch (start us, length us, event | category | flops | bytes accessed | tf_op | source)
XLA Modules:
  0.0 1603.9 jit_solution(10749047523685592035)
XLA Ops:
  10.8 15.1 all-gather.5.cloned.1.call-done
  31.4 3.6 multiply_convert_fusion.3
  35.1 3.5 collective-permute-start
  41.2 3.1 collective-permute-done.1
  44.7 10.8 fusion.94
  58.2 7.0 fusion.93
  67.7 25.7 %fusion.39 = (f32[768]{0:T(1024)S(1)}, f32[768]{0:T(1024)S(1)}, f32[768]{0:T(1024)S(1)}, f32[768]{0:T(1024)S(1)}, f32[768]{0:T(1024)S(1)}, /*index=5*/f32[768]{0...) fusion(f32[798,768]{1,0:T(8,128)} %copy-done.1, ...), kind=kLoop, calls=%fused_computation.77 | loop fusion | flops 25938432 | bytes 48433152 | tf_op jit(solution)/shard_map/reduce_sum | solution.py:81
  93.4 3.9 fusion.38
  116.1 5.4 stack.127
  121.6 4.0 collective-permute-start.2
  126.9 6.3 convolution_convert_fusion
  135.2 10.9 multiply_convert_fusion
  148.5 3.6 add_convert_fusion
  154.8 6.8 fusion.72
  162.3 6.1 fusion.88
  169.7 6.3 fusion.86
  176.0 4.4 fusion.1
  183.0 4.0 reduce-scatter.8.cloned.1.call-done
  189.5 3.1 all-reduce
  193.3 3.6 fusion.81
  196.9 312.4 %all-reduce.8.cloned.1.call-done = f32[31,768]{1,0:T(8,128)} async-done(((f32[31,768]{1,0:T(8,128)}), f32[31,768]{1,0:T(8,128)}) %all-reduce.8.cloned.1.call-update) | async-done | bytes 95248 | tf_op jit(solution)/shard_map/psum | solution.py:92
  509.3 364.8 %reduce-scatter.14.cloned.1.call-done = f32[768,24]{0,1:T(8,128)} async-done(((f32[768,1536]{0,1:T(8,128)}), f32[768,24]{0,1:T(8,128)}) %reduce-scatter.14.cloned.1.call-update) | async-done | bytes 73744 | tf_op jit(solution)/shard_map/reduce_scatter | solution.py:118
  874.1 360.9 %reduce-scatter.10.cloned.1.call-done = f32[24,768]{1,0:T(8,128)} async-done(((f32[1536,768]{1,0:T(8,128)}), f32[24,768]{1,0:T(8,128)}) %reduce-scatter.10.cloned.1.call-update) | async-done | bytes 73744 | tf_op jit(solution)/shard_map/reduce_scatter | solution.py:116
  1235.0 360.9 %reduce-scatter.12.cloned.1.call-done = f32[24,768]{1,0:T(8,128)} async-done(((f32[1536,768]{1,0:T(8,128)}), f32[24,768]{1,0:T(8,128)}) %reduce-scatter.12.cloned.1.call-update) | async-done | bytes 73744 | tf_op jit(solution)/shard_map/reduce_scatter | solution.py:117
  (237 shorter events, 52.4 us)
Async XLA Ops:
  7.2 24.2 %copy-start = (bf16[1536,768]{1,0:T(8,128)(2,1)S(1)}, bf16[1536,768]{1,0:T(8,128)(2,1)}, u32[]{:S(2)}) copy-start(bf16[1536,768]{1,0:T(8,128)(2,1)} %param.10) | copy-start | bytes 7077892
  7.2 18.6 %all-gather.5.cloned.1.call-start = ((), (), s32[]{:S(2)}) async-start(), calls=%async_computation.12 | async-start | bytes 3538944 | tf_op jit(solution)/shard_map/all_gather | solution.py:40
  7.9 50.2 %all-gather.7.cloned.1.call-start = ((), (), s32[]{:S(2)}) async-start(), calls=%async_computation.13 | async-start | bytes 3538944 | tf_op jit(solution)/shard_map/all_gather | solution.py:66
  8.7 146.1 %all-reduce.6.cloned.1.call-start = ((), (), s32[]{:S(2)}) async-start(), calls=%async_computation.9 | async-start | bytes 196608 | tf_op jit(solution)/shard_map/psum | solution.py:92
  9.4 19.5 %copy-start.10 = (f32[31,768]{1,0:T(8,128)}, f32[31,768]{1,0:T(8,128)S(1)}, u32[]{:S(2)}) copy-start(f32[31,768]{1,0:T(8,128)S(1)} %convert_element_type.70) | copy-start | bytes 285700
  35.1 6.1 collective-permute-start
  38.6 5.7 collective-permute-start.1
  41.1 14.4 copy-start.44
  41.1 14.4 copy-start.46
  41.1 14.4 copy-start.48
  41.1 14.4 copy-start.50
  41.1 14.4 copy-start.52
  41.1 14.4 copy-start.54
  41.2 14.4 copy-start.56
  41.2 14.4 copy-start.58
  67.6 25.7 %copy-start.2 = (f32[798,768]{1,0:T(8,128)S(1)}, f32[798,768]{1,0:T(8,128)}, u32[]{:S(2)}) copy-start(f32[798,768]{1,0:T(8,128)} %copy-done.1) | copy-start | bytes 7354372
  121.6 58.9 %reduce-scatter.6.cloned.1.call-start = ((), (), s32[]{:S(2)}) async-start(), calls=%async_computation.5 | async-start | bytes 3538944 | tf_op jit(solution)/shard_map/reduce_scatter | solution.py:61
  121.6 11.9 collective-permute-start.2
  125.6 7.9 collective-permute-start.3
  133.2 53.8 %reduce-scatter.8.cloned.1.call-start = ((), (), s32[]{:S(2)}) async-start(), calls=%async_computation.6 | async-start | bytes 3538944 | tf_op jit(solution)/shard_map/reduce_scatter | solution.py:96
  152.1 357.2 %all-reduce.8.cloned.1.call-start = ((), (), s32[]{:S(2)}) async-start(), calls=%async_computation.10 | async-start | bytes 196608 | tf_op jit(solution)/shard_map/psum | solution.py:92
  154.8 719.4 %reduce-scatter.14.cloned.1.call-start = ((), (), s32[]{:S(2)}) async-start(), calls=%async_computation.11 | async-start | bytes 4792320 | tf_op jit(solution)/shard_map/reduce_scatter | solution.py:118
  161.7 1073.3 %reduce-scatter.10.cloned.1.call-start = ((), (), s32[]{:S(2)}) async-start(), calls=%async_computation.7 | async-start | bytes 4792320 | tf_op jit(solution)/shard_map/reduce_scatter | solution.py:116
  168.4 1427.5 %reduce-scatter.12.cloned.1.call-start = ((), (), s32[]{:S(2)}) async-start(), calls=%async_computation.8 | async-start | bytes 4792320 | tf_op jit(solution)/shard_map/reduce_scatter | solution.py:117
  (67 other events, 321.5 us)
Sparse Core Ops, SparseCore 0:
  9.7 16.1 all-gather.4
  27.5 14.9 all-gather.6
  121.7 32.9 all-reduce.5
  156.9 13.6 reduce-scatter.5
  172.9 14.0 reduce-scatter.7
  189.3 319.9 all-reduce.7
  512.3 361.8 reduce-scatter.13
  877.1 357.8 reduce-scatter.9
  1238.0 357.8 reduce-scatter.11
